TPU v7x, 32 devices: a whole 2x2x4 slice. The times are simulated.
32 devices in a mesh: strip: 8 (over z, y), panel: 4 (over x, core).
Axes of the slice: x: 2, y: 2, z: 4, core: 2. Of those that a mesh axis runs over, the one named last changes fastest.
Arguments:
- h_cond: float32 [32, 256], P('strip', 'panel'), may hold values from 0.3 to 3
- v_cond: float32 [32, 256], P('strip', 'panel'), may hold values from 0.3 to 3
- confidence: float32 [32, 256], P('strip', 'panel'), may hold values from 1.8e-05 to 0.00225
- teacher: float32 [16, 32, 256], P(None, 'strip', 'panel'), may hold values from -6 to 6
- grad_x: float32 [16, 32, 256], P(None, 'strip', 'panel'), may hold values from -4 to 4
- grad_y: float32 [16, 32, 256], P(None, 'strip', 'panel'), may hold values from -4 to 4
Outputs:
- depth: float32 [16, 32, 256], P(None, 'strip', 'panel')
All inputs are finite; a program needn't handle non-finite values.
Results may differ from a plain program's by a relative error of at most 0.0003.
Values sent between devices are 32-bit elements; how exact they have to be, the bound alone decides.
A program may use at most 320 MiB of HBM per device.

v0:
```python
import jax
import jax.numpy as jnp
from jax import lax
from jax.sharding import PartitionSpec as P

HIGH = lax.Precision.HIGHEST


def shifted(value, axis, by):
    count = lax.axis_size(axis)
    pairs = [(i, i + by) for i in range(count) if 0 <= i + by < count]
    return lax.ppermute(value, axis, pairs)


def carried_in(value, axis, join, neutral, backward):
    count, mine = (lax.axis_size(axis), lax.axis_index(axis))
    pieces = jax.tree.map(lambda part: lax.all_gather(part, axis), value)
    if backward:
        pieces = jax.tree.map(lambda part: part[::-1], pieces)
        mine = count - 1 - mine
    total = jax.tree.map(
        lambda part, zero: jnp.full_like(part, 0) + jnp.asarray(zero, part.dtype), value, neutral
    )

    def turn(position, total):
        longer = join(total, jax.tree.map(lambda part: part[position], pieces))
        return jax.tree.map(lambda new, old: jnp.where(position < mine, new, old), longer, total)

    return lax.fori_loop(0, count - 1, turn, total)


def product(left, right):
    return jnp.dot(left, right, precision=HIGH, preferred_element_type=jnp.float32)


def apply_to(matrix, vectors):
    return product(vectors, matrix.T)


def row_matrix(diag_row, link_row):
    extent = diag_row.shape[0]
    row_ids = lax.broadcasted_iota(jnp.int32, (extent, extent), 0)
    col_ids = lax.broadcasted_iota(jnp.int32, (extent, extent), 1)
    east = col_ids == (row_ids + 1) % extent
    west = row_ids == (col_ids + 1) % extent
    link = jnp.where(east, link_row[:, None], 0.0) + jnp.where(west, link_row[None, :], 0.0)
    return jnp.where(row_ids == col_ids, diag_row[:, None], 0.0) - link


def inverse(matrix):
    factor = jnp.linalg.cholesky(matrix)
    return jax.scipy.linalg.cho_solve((factor, True), jnp.eye(matrix.shape[0], dtype=jnp.float32))


def load_update(factor, upper, lower):
    vector = jax.scipy.linalg.cho_solve((factor, True), (upper[4] + lower[3]).T)
    return (upper[3] - product(upper[1], vector).T, lower[4] - product(lower[1].T, vector).T)


def merge_whole(upper, lower):
    extent = upper[2].shape[0]
    factor = jnp.linalg.cholesky(upper[2] + lower[0])
    solved = jax.scipy.linalg.cho_solve(
        (factor, True), jnp.concatenate([upper[1].T, lower[1]], axis=1)
    )
    first_cols = solved[:, :extent]
    second_cols = solved[:, extent:]
    first_load, second_load = load_update(factor, upper, lower)
    return (
        upper[0] - product(upper[1], first_cols),
        -product(upper[1], second_cols),
        lower[2] - product(lower[1].T, second_cols),
        first_load,
        second_load,
    )


def merge_flagged(upper, lower):
    merged = merge_whole(upper[:5], lower[:5])
    upper_empty = upper[5] > 0.5
    lower_empty = lower[5] > 0.5
    picked = tuple(
        (
            jnp.where(upper_empty, lower_part, jnp.where(lower_empty, upper_part, merged_part))
            for upper_part, lower_part, merged_part in zip(upper[:5], lower[:5], merged)
        )
    )
    return picked + (upper[5] * lower[5],)


def chain_maps(earlier_map, later_map):
    return (
        product(later_map[0], earlier_map[0]),
        later_map[1] + apply_to(later_map[0], earlier_map[1]),
    )


def substitute(value_below, inputs):
    gain, offset = inputs
    value = offset + apply_to(gain, value_below)
    return (value, value)


def shards(h_cond, v_cond, confidence, teacher, grad_x, grad_y):
    slice_cols = h_cond.shape[1]
    local_rows = h_cond.shape[0]
    hypotheses = teacher.shape[0]
    edge_rows = jnp.concatenate([v_cond[-1][None], v_cond[-1][None] * grad_y[:, -1]], axis=0)
    above = shifted(edge_rows, "strip", 1)
    packed = jnp.concatenate(
        [
            h_cond,
            v_cond,
            confidence,
            above,
            teacher.reshape(hypotheses * local_rows, slice_cols),
            grad_x.reshape(hypotheses * local_rows, slice_cols),
            grad_y.reshape(hypotheses * local_rows, slice_cols),
        ],
        axis=0,
    )
    whole = lax.all_gather(packed, "panel", axis=1, tiled=True)
    extent = whole.shape[1]
    horizontal = whole[:local_rows]
    vertical = whole[local_rows : 2 * local_rows]
    weights = whole[2 * local_rows : 3 * local_rows]
    vertical_edge = whole[3 * local_rows]
    flux_edge = whole[3 * local_rows + 1 : 3 * local_rows + 1 + hypotheses]
    base = 3 * local_rows + 1 + hypotheses
    stride = hypotheses * local_rows
    targets = whole[base : base + stride].reshape(hypotheses, local_rows, extent)
    slope_x = whole[base + stride : base + 2 * stride].reshape(hypotheses, local_rows, extent)
    slope_y = whole[base + 2 * stride : base + 3 * stride].reshape(hypotheses, local_rows, extent)
    vertical_above = jnp.concatenate([vertical_edge[None], vertical[:-1]], axis=0)
    flux = vertical[None] * slope_y
    flux_above = jnp.concatenate([flux_edge[:, None], flux[:, :-1]], axis=1)
    along = horizontal[None] * slope_x
    loads = weights[None] * targets + jnp.roll(along, 1, axis=2) - along + flux_above - flux
    loads = jnp.transpose(loads, (1, 0, 2))
    diagonal = jnp.roll(horizontal, 1, axis=1) + horizontal + vertical_above + vertical + weights
    blocks = jax.vmap(row_matrix)(diagonal, horizontal)
    zeros_mat = jnp.zeros((extent, extent), jnp.float32)
    zeros_vec = jnp.zeros((hypotheses, extent), jnp.float32)
    identity = jnp.eye(extent, dtype=jnp.float32)
    start = (zeros_mat, -jnp.diag(vertical_above[0]), blocks[0], zeros_vec, loads[0])

    def fold_step(segment, inputs):
        matrix_row, coupling, load_row = inputs
        piece = (zeros_mat, -jnp.diag(coupling), matrix_row, zeros_vec, load_row)
        merged = merge_whole(segment, piece)
        return (merged, None)

    segment, _ = lax.scan(fold_step, start, (blocks[1:], vertical_above[1:], loads[1:]))
    filled = segment + (jnp.zeros((), jnp.float32),)
    blank = (zeros_mat, zeros_mat, identity, zeros_vec, zeros_vec, jnp.ones((), jnp.float32))
    prefix = carried_in(filled, "strip", merge_flagged, blank, False)
    prefix_matrix, prefix_load = (prefix[2], prefix[4])

    def eliminate(state, inputs):
        inverse_prev, load_prev, pivot_prev = state
        matrix_row, coupling, load_row, coupling_below = inputs
        pivot = matrix_row - coupling[:, None] * inverse_prev * coupling[None, :]
        carried = load_row + coupling[None, :] * apply_to(inverse_prev, load_prev)
        inverse_now = inverse(pivot)
        return (
            (inverse_now, carried, pivot),
            (inverse_now * coupling_below[None, :], apply_to(inverse_now, carried)),
        )

    final_state, (gains, offsets) = lax.scan(
        eliminate,
        (inverse(prefix_matrix), prefix_load, identity),
        (blocks, vertical_above, loads, vertical),
    )

    def compose(mapping, inputs):
        gain, offset = inputs
        return ((product(gain, mapping[0]), offset + apply_to(gain, mapping[1])), None)

    (reach, moved), _ = lax.scan(compose, (identity, zeros_vec), (gains, offsets), reverse=True)
    beyond = carried_in((reach, moved), "strip", chain_maps, (identity, zeros_vec), True)
    _, solution = lax.scan(substitute, beyond[1], (gains, offsets), reverse=True)
    solution = jnp.transpose(solution, (1, 0, 2))
    return lax.dynamic_slice_in_dim(solution, lax.axis_index("panel") * slice_cols, slice_cols, 2)


def solution(mesh):
    in_specs = (
        P("strip", "panel"),
        P("strip", "panel"),
        P("strip", "panel"),
        P(None, "strip", "panel"),
        P(None, "strip", "panel"),
        P(None, "strip", "panel"),
    )
    out_specs = P(None, "strip", "panel")
    return jax.shard_map(shards, mesh=mesh, in_specs=in_specs, out_specs=out_specs, check_vma=False)
```

profile of v0, /device:TPU:0, one launch (start us, length us, event | category | flops | bytes accessed | tf_op | source)
XLA Modules:
  0.0 1301.3 jit_solution(6325950305121923464)
XLA Ops:
  29.9 212.2 %while.121 = (s32[]{:T(128)}, f32[256,256]{0,1:T(8,128)S(1)}, f32[256,256]{0,1:T(8,128)S(1)}, f32[256,256]{1,0:T(8,128)S(1)}, f32[16,256]{1,0:T(8,128)}, /*index...) while((s32[]{:T(128)}, f32[256,256]{0,1:T(8,128)S(1)}, ...), condition=%wide.region_5.9_spmd.clone, body=%wide.region_0.8_spmd.clone.sunk | while | flops 1304207616 | bytes 12901723 | solution.py:153
  30.6 11.7 cholesky.697
  52.6 11.7 cholesky.699
  70.5 19.7 %custom-call.64 = f32[2,128,128]{1,2,0:T(8,128)S(1)} custom-call(f32[2,128,128]{2,1,0:T(8,128)S(1)} %get-tuple-element.1646), custom_call_target="InvertDiagBlocksLowerTriangular" | custom-call | tf_op jit(solution)/shard_map/while/body/eval_jaxpr/jit(_cho_solve)/triangular_solve | solution.py:63
  100.6 11.7 cholesky.697
  122.7 11.7 cholesky.699
  140.5 19.7 %custom-call.64 = f32[2,128,128]{1,2,0:T(8,128)S(1)} custom-call(f32[2,128,128]{2,1,0:T(8,128)S(1)} %get-tuple-element.1646), custom_call_target="InvertDiagBlocksLowerTriangular" | custom-call | tf_op jit(solution)/shard_map/while/body/eval_jaxpr/jit(_cho_solve)/triangular_solve | solution.py:63
  171.3 11.7 cholesky.697
  193.4 11.7 cholesky.699
  211.3 19.7 %custom-call.64 = f32[2,128,128]{1,2,0:T(8,128)S(1)} custom-call(f32[2,128,128]{2,1,0:T(8,128)S(1)} %get-tuple-element.1646), custom_call_target="InvertDiagBlocksLowerTriangular" | custom-call | tf_op jit(solution)/shard_map/while/body/eval_jaxpr/jit(_cho_solve)/triangular_solve | solution.py:63
  246.6 22.9 %all-reduce.1 = f32[8]{0:T(128)S(1)} all-reduce(f32[8]{0:T(128)S(1)} %dynamic-update-slice.15), channel_id=1, replica_groups=mesh['strip'=8,'panel'=4] {'strip'}, use_global_device_ids=true, to_apply=%add.1 | all-reduce | flops 8 | bytes 64
  269.7 31.3 %all-gather.3 = f32[128,256]{1,0:T(8,128)S(1)} all-gather(f32[16,256]{1,0:T(8,128)} %get-tuple-element.612), channel_id=5, replica_groups=mesh['strip'=8,'panel'=4] {'strip'}, dimensions={0}, use_global_device_ids=true | all-gather | bytes 147456 | tf_op jit(solution)/shard_map/all_gather | solution.py:17
  301.0 33.1 %all-gather.4 = f32[128,256]{1,0:T(8,128)} all-gather(f32[16,256]{1,0:T(8,128)S(1)} %copy-done.4), channel_id=6, replica_groups=mesh['strip'=8,'panel'=4] {'strip'}, dimensions={0}, use_global_device_ids=true | all-gather | bytes 147456 | tf_op jit(solution)/shard_map/all_gather | solution.py:17
  346.6 49.9 %all-gather.16.cloned.1.call-done = f32[2048,256]{1,0:T(8,128)} async-done(((f32[256,256]{1,0:T(8,128)}), f32[2048,256]{1,0:T(8,128)}) %all-gather.16.cloned.1.call-update) | async-done | bytes 2097168 | tf_op jit(solution)/shard_map/all_gather | solution.py:17
  396.4 508.2 %while.123 = (s32[]{:T(128)}, f32[256,256]{0,1:T(8,128)}, f32[256,256]{0,1:T(8,128)S(1)}, f32[16,256]{1,0:T(8,128)S(1)}, f32[]{:T(128)}, /*index=5*/s32[]{:T(128...) while((s32[]{:T(128)}, f32[256,256]{0,1:T(8,128)}, ...), condition=%wide.region_7.11_spmd.clone, body=%wide.region_6.10_spmd.clone.sunk | while | flops 1090179328 | bytes 17074636 | solution.py:29
  397.8 11.7 cholesky.723
  419.8 11.7 cholesky.725
  437.5 19.7 %custom-call.67 = f32[2,128,128]{1,2,0:T(8,128)S(1)} custom-call(f32[2,128,128]{2,1,0:T(8,128)S(1)} %get-tuple-element.1668), custom_call_target="InvertDiagBlocksLowerTriangular" | custom-call | tf_op jit(solution)/shard_map/while/body/eval_jaxpr/jit(_cho_solve)/triangular_solve | solution.py:63
  470.3 11.7 cholesky.723
  492.4 11.7 cholesky.725
  510.0 19.7 %custom-call.67 = f32[2,128,128]{1,2,0:T(8,128)S(1)} custom-call(f32[2,128,128]{2,1,0:T(8,128)S(1)} %get-tuple-element.1668), custom_call_target="InvertDiagBlocksLowerTriangular" | custom-call | tf_op jit(solution)/shard_map/while/body/eval_jaxpr/jit(_cho_solve)/triangular_solve | solution.py:63
  542.9 11.7 cholesky.723
  564.9 11.7 cholesky.725
  582.6 19.7 %custom-call.67 = f32[2,128,128]{1,2,0:T(8,128)S(1)} custom-call(f32[2,128,128]{2,1,0:T(8,128)S(1)} %get-tuple-element.1668), custom_call_target="InvertDiagBlocksLowerTriangular" | custom-call | tf_op jit(solution)/shard_map/while/body/eval_jaxpr/jit(_cho_solve)/triangular_solve | solution.py:63
  615.4 11.7 cholesky.723
  637.5 11.7 cholesky.725
  655.1 19.7 %custom-call.67 = f32[2,128,128]{1,2,0:T(8,128)S(1)} custom-call(f32[2,128,128]{2,1,0:T(8,128)S(1)} %get-tuple-element.1668), custom_call_target="InvertDiagBlocksLowerTriangular" | custom-call | tf_op jit(solution)/shard_map/while/body/eval_jaxpr/jit(_cho_solve)/triangular_solve | solution.py:63
  687.9 11.7 cholesky.723
  710.0 11.7 cholesky.725
  727.7 19.7 %custom-call.67 = f32[2,128,128]{1,2,0:T(8,128)S(1)} custom-call(f32[2,128,128]{2,1,0:T(8,128)S(1)} %get-tuple-element.1668), custom_call_target="InvertDiagBlocksLowerTriangular" | custom-call | tf_op jit(solution)/shard_map/while/body/eval_jaxpr/jit(_cho_solve)/triangular_solve | solution.py:63
  760.5 11.7 cholesky.723
  782.6 11.7 cholesky.725
  800.2 19.7 %custom-call.67 = f32[2,128,128]{1,2,0:T(8,128)S(1)} custom-call(f32[2,128,128]{2,1,0:T(8,128)S(1)} %get-tuple-element.1668), custom_call_target="InvertDiagBlocksLowerTriangular" | custom-call | tf_op jit(solution)/shard_map/while/body/eval_jaxpr/jit(_cho_solve)/triangular_solve | solution.py:63
  855.1 11.7 cholesky.725
  872.8 19.7 %custom-call.67 = f32[2,128,128]{1,2,0:T(8,128)S(1)} custom-call(f32[2,128,128]{2,1,0:T(8,128)S(1)} %get-tuple-element.1668), custom_call_target="InvertDiagBlocksLowerTriangular" | custom-call | tf_op jit(solution)/shard_map/while/body/eval_jaxpr/jit(_cho_solve)/triangular_solve | solution.py:63
  926.9 11.7 cholesky.333
  946.6 20.5 %custom-call.44 = f32[2,128,128]{1,2,0:T(8,128)S(1)} custom-call(f32[2,128,128]{2,1,0:T(8,128)} %get-tuple-element.774), custom_call_target="InvertDiagBlocksLowerTriangular" | custom-call | tf_op jit(solution)/shard_map/jit(_cho_solve)/triangular_solve | solution.py:52
  968.9 259.3 %while.118 = (s32[]{:T(128)}, f32[256,256]{1,0:T(8,128)S(1)}, f32[16,256]{1,0:T(8,128)S(1)}, f32[4,256,256]{2,1,0:T(8,128)S(1)}, f32[4,16,256]{2,1,0:T(8,128)S(1...) while((s32[]{:T(128)}, f32[256,256]{1,0:T(8,128)S(1)}, ...), condition=%wide.region_9.14_spmd, body=%wide.region_8.13_spmd.sunk | while | flops 378560768 | bytes 9528664 | solution.py:170
  992.5 11.7 cholesky.669
  1010.8 19.7 %custom-call.61 = f32[2,128,128]{1,2,0:T(8,128)S(1)} custom-call(f32[2,128,128]{2,1,0:T(8,128)S(1)} %get-tuple-element.1620), custom_call_target="InvertDiagBlocksLowerTriangular" | custom-call | tf_op jit(solution)/shard_map/while/body/eval_jaxpr/jit(_cho_solve)/triangular_solve | solution.py:52
  1057.3 11.7 cholesky.669
  1075.6 19.7 %custom-call.61 = f32[2,128,128]{1,2,0:T(8,128)S(1)} custom-call(f32[2,128,128]{2,1,0:T(8,128)S(1)} %get-tuple-element.1620), custom_call_target="InvertDiagBlocksLowerTriangular" | custom-call | tf_op jit(solution)/shard_map/while/body/eval_jaxpr/jit(_cho_solve)/triangular_solve | solution.py:52
  1122.0 11.7 cholesky.669
  1140.4 19.7 %custom-call.61 = f32[2,128,128]{1,2,0:T(8,128)S(1)} custom-call(f32[2,128,128]{2,1,0:T(8,128)S(1)} %get-tuple-element.1620), custom_call_target="InvertDiagBlocksLowerTriangular" | custom-call | tf_op jit(solution)/shard_map/while/body/eval_jaxpr/jit(_cho_solve)/triangular_solve | solution.py:52
  1186.8 11.7 cholesky.669
  1205.2 19.7 %custom-call.61 = f32[2,128,128]{1,2,0:T(8,128)S(1)} custom-call(f32[2,128,128]{2,1,0:T(8,128)S(1)} %get-tuple-element.1620), custom_call_target="InvertDiagBlocksLowerTriangular" | custom-call | tf_op jit(solution)/shard_map/while/body/eval_jaxpr/jit(_cho_solve)/triangular_solve | solution.py:52
  1232.1 31.1 %all-gather.5 = f32[128,256]{1,0:T(8,128)S(1)} all-gather(f32[16,256]{1,0:T(8,128)S(1)} %get-tuple-element.618), channel_id=7, replica_groups=mesh['strip'=8,'panel'=4] {'strip'}, dimensions={0}, use_global_device_ids=true | all-gather | bytes 147456 | tf_op jit(solution)/shard_map/all_gather | solution.py:17
  1263.2 16.6 %all-gather.18.cloned.1.call-done = f32[2048,256]{1,0:T(8,128)} async-done(((f32[256,256]{1,0:T(8,128)}), f32[2048,256]{1,0:T(8,128)}) %all-gather.18.cloned.1.call-update) | async-done | bytes 2097168 | tf_op jit(solution)/shard_map/all_gather | solution.py:17
  (791 shorter events, 565.3 us)
Async XLA Ops:
  6.5 327.6 %all-gather.12.cloned.1.call-start = ((), (), s32[]{:S(2)}) async-start(), calls=%async_computation | async-start | bytes 2359296 | tf_op jit(solution)/shard_map/all_gather | solution.py:17
  8.0 6.3 collective-permute-start
  24.6 4.0 copy-start.5
  25.4 3.2 copy-start.3
  242.1 0.7 copy-start.2
  242.1 1.7 copy-start
  242.1 58.9 %copy-start.4 = (f32[16,256]{1,0:T(8,128)S(1)}, f32[16,256]{1,0:T(8,128)}, u32[]{:S(2)}) copy-start(f32[16,256]{1,0:T(8,128)} %get-tuple-element.613) | copy-start | bytes 49156
  242.8 103.8 %all-gather.14.cloned.1.call-start = ((), (), s32[]{:S(2)}) async-start(), calls=%async_computation.1 | async-start | bytes 2359296 | tf_op jit(solution)/shard_map/all_gather | solution.py:17
  243.7 152.7 %all-gather.16.cloned.1.call-start = ((), (), s32[]{:S(2)}) async-start(), calls=%async_computation.2 | async-start | bytes 2359296 | tf_op jit(solution)/shard_map/all_gather | solution.py:17
  244.5 1035.3 %all-gather.18.cloned.1.call-start = ((), (), s32[]{:S(2)}) async-start(), calls=%async_computation.3 | async-start | bytes 2359296 | tf_op jit(solution)/shard_map/all_gather | solution.py:17
  1231.4 0.7 copy-start.1
Sparse Core Ops, SparseCore 0:
  242.9 53.6 all-gather.11
  298.7 47.7 all-gather.13
  348.7 47.6 all-gather.15
  1232.2 47.5 all-gather.17
where the time goes:
time: 1310 us; the launch traced here: 1300 us
  other arithmetic  818 us (62%)
  local copies, waits for them, and re-layouts  131 us (10%)
  blocking collectives  124 us (9%)
  matrix products  97 us (7%)
  waiting for transfers between devices  77.8 us (6%)
  loops' own time  32.6 us (2%)
  between operations  15.2 us (1%)
    another operation x60, other arithmetic, merge_whole(): factor = jnp.linalg.cholesky(upper[2] + lower[0])  340 us
    another operation x40, other arithmetic, merge_whole(): jax.scipy.linalg.cho_solve((factor, True), jnp.concatenate([upper[1].T, l...  197 us
    another operation x35, other arithmetic, inverse(): factor = jnp.linalg.cholesky(matrix)  173 us
    another operation x21, other arithmetic, inverse(): jax.scipy.linalg.cho_solve((factor, True), jnp.eye(matrix.shape[0], dtype...  99.4 us
    all_gather x3, blocking collectives, carried_in(): pieces = jax.tree.map(lambda part: lax.all_gather(part, axis), value)  95.5 us
    all_gather x4, waiting for transfers between devices, carried_in(): pieces = jax.tree.map(lambda part: lax.all_gather(part, axis), value)  76 us
    dot_general x63, matrix products, product(): jnp.dot(left, right, precision=HIGH, preferred_element_type=jnp.float32)  42.2 us
    another operation x70, local copies, waits for them, and re-layouts, merge_whole(): jax.scipy.linalg.cho_solve((factor, True), jnp.concatenate([upper[1].T, l...  39 us
  transfers between devices with their start and end apart: 5, of which 4 were waited for; matrix products, arithmetic and copies ran while one was open for 0% of the time, Pallas kernels for 0%

commit v1 on v0

--- a/solution.py
+++ b/solution.py
@@ -1,6 +1,10 @@
+import functools
+
 import jax
 import jax.numpy as jnp
 from jax import lax
+from jax.experimental import pallas as pl
+from jax.experimental.pallas import tpu as pltpu
 from jax.sharding import PartitionSpec as P
 
 HIGH = lax.Precision.HIGHEST
@@ -101,7 +105,7 @@
     return (value, value)
 
 
-def shards(h_cond, v_cond, confidence, teacher, grad_x, grad_y):
+def latitude_shards(h_cond, v_cond, confidence, teacher, grad_x, grad_y):
     slice_cols = h_cond.shape[1]
     local_rows = h_cond.shape[0]
     hypotheses = teacher.shape[0]
@@ -184,6 +188,210 @@
     return lax.dynamic_slice_in_dim(solution, lax.axis_index("panel") * slice_cols, slice_cols, 2)
 
 
+def lane_block(shape, rows):
+    return lax.broadcasted_iota(jnp.int32, shape, 1) // rows
+
+
+def eliminate_column(systems, rows, group):
+    row_ids = lax.broadcasted_iota(jnp.int32, systems[0].shape, 0)
+    shape = systems[0].shape
+    systems = list(systems)
+    for first in range(0, rows, group):
+        columns = [
+            [jnp.broadcast_to(m[:, rows + first + t : rows + first + t + 1], shape) for t in range(group)]
+            for m in systems
+        ]
+        for t in range(group):
+            k = first + t
+            for b in range(len(systems)):
+                column = columns[b][t]
+                scale = 1.0 / column[k : k + 1]
+                pivot = systems[b][k : k + 1] * scale
+                systems[b] = jnp.where(row_ids == k, pivot, systems[b] - column * pivot)
+                for u in range(t + 1, group):
+                    later = columns[b][u]
+                    part = later[k : k + 1] * scale
+                    columns[b][u] = jnp.where(row_ids == k, part, later - column * part)
+    return systems
+
+
+def merge_segments(tops, bottoms, rows):
+    pairs = len(tops) // 2
+    group = max(1, 4 // pairs)
+    lanes = tops[0].shape[1]
+    block = lane_block(tops[0].shape, rows)
+    zero = jnp.zeros((rows, lanes), jnp.float32)
+    solved = eliminate_column(
+        [bottoms[2 * i] + tops[2 * i + 1] for i in range(pairs)], rows, group
+    )
+    new_tops, new_bottoms = [], []
+    for i, x in enumerate(solved):
+        x_top = jnp.where(block == 0, 0.0, jnp.where(block == 1, pltpu.roll(x, rows, 1), x))
+        x_bottom = jnp.where(block == 2, 0.0, jnp.where(block == 1, pltpu.roll(x, lanes - rows, 1), x))
+        right = jnp.concatenate([x_bottom, zero, x_top, zero], axis=0)
+        west, east = tops[2 * i], bottoms[2 * i + 1]
+        change = product(jnp.concatenate([west, east], axis=0), right)
+        new_tops.append(jnp.where(block == 2, 0.0, west) - change[:rows])
+        new_bottoms.append(jnp.where(block == 0, 0.0, east) - change[rows:])
+    return solved, new_tops, new_bottoms
+
+
+def merge_tree(tops, bottoms, rows, kept_ref):
+    position = 0
+    while len(tops) > 1:
+        solved, tops, bottoms = merge_segments(tops, bottoms, rows)
+        for x in solved:
+            kept_ref[position] = x
+            position += 1
+    return tops[0], bottoms[0]
+
+
+def middle(x, west, east, rows):
+    zero = jnp.zeros_like(x)
+    right = jnp.concatenate([west, zero, east, zero], axis=0)
+    return jnp.where(lane_block(x.shape, rows) == 3, x - product(x, right), 0.0)
+
+
+def descend(kept_ref, leaves, leaf, west, east, rows):
+    position, count = leaves - 2, 1
+    while count < leaves:
+        held = kept_ref[position + (leaf * count) // leaves]
+        mid = middle(held, west, east, rows)
+        go_east = ((leaf * 2 * count) // leaves) % 2 == 1
+        west, east = jnp.where(go_east, mid, west), jnp.where(go_east, east, mid)
+        count *= 2
+        position -= count
+    return west, east
+
+
+def local_kernel(fields_ref, segment_ref, kept_ref, *, rows, maps):
+    count, _, lanes = fields_ref.shape
+    shape = (rows, lanes)
+    block = lane_block(shape, rows)
+    lane = lax.broadcasted_iota(jnp.int32, shape, 1)
+    row = lax.broadcasted_iota(jnp.int32, shape, 0)
+    diag0, diag1, diag2 = lane == row, lane == row + rows, lane == row + 2 * rows
+    upper, lower = lane == row + rows + 1, lane == row + rows - 1
+    upper = jnp.logical_and(upper, block == 1)
+    lower = jnp.logical_and(lower, block == 1)
+    load_lane = jnp.logical_and(lane >= 3 * rows, lane < 3 * rows + maps)
+    tops, bottoms = [], []
+    for j in range(count):
+        f = fields_ref[j]
+        above = jnp.where(row == 0, 0.0, pltpu.roll(f, 1, 0))
+        h = jnp.broadcast_to(f[:, 0:1], shape)
+        v = jnp.broadcast_to(f[:, 1:2], shape)
+        w = jnp.broadcast_to(f[:, 2:3], shape)
+        va = jnp.broadcast_to(above[:, 1:2], shape)
+        flux_above = pltpu.roll(above, 2 * rows, 1)
+        along = pltpu.roll(f, rows, 1)
+        top = (
+            jnp.where(diag1, h + va + v + w, 0.0)
+            - jnp.where(upper, v, 0.0)
+            - jnp.where(lower, va, 0.0)
+            - jnp.where(diag2, h, 0.0)
+            + jnp.where(load_lane, f + flux_above, 0.0)
+        )
+        bottom = jnp.where(diag1, h, 0.0) - jnp.where(diag0, h, 0.0) + jnp.where(load_lane, along, 0.0)
+        tops.append(top)
+        bottoms.append(bottom)
+    top, bottom = merge_tree(tops, bottoms, rows, kept_ref)
+    segment_ref[0:rows] = top
+    segment_ref[rows : 2 * rows] = bottom
+
+
+def group_kernel(segments_ref, segment_ref, kept_ref, *, rows):
+    count = segments_ref.shape[0]
+    tops = [segments_ref[i, 0:rows] for i in range(count)]
+    bottoms = [segments_ref[i, rows : 2 * rows] for i in range(count)]
+    top, bottom = merge_tree(tops, bottoms, rows, kept_ref)
+    segment_ref[0:rows] = top
+    segment_ref[rows : 2 * rows] = bottom
+
+
+def final_kernel(
+    where_ref, segments_ref, kept_local_ref, kept_strip_ref, values_ref, kept_panel_ref, *, rows, strips, panels
+):
+    lanes = segments_ref.shape[2]
+    block = lane_block((rows, lanes), rows)
+    tops = [segments_ref[i, 0:rows] for i in range(panels)]
+    bottoms = [segments_ref[i, rows : 2 * rows] for i in range(panels)]
+    top, bottom = merge_tree(tops, bottoms, rows, kept_panel_ref)
+    wrap = pltpu.roll(top, lanes - rows, 1) + pltpu.roll(bottom, rows, 1)
+    closing = top + bottom + jnp.where(block == 1, wrap, 0.0)
+    first = eliminate_column([closing], rows, 4)[0]
+    first = jnp.where(block == 3, first, 0.0)
+    west, east = descend(kept_panel_ref, panels, where_ref[1], first, first, rows)
+    west, east = descend(kept_strip_ref, strips, where_ref[0], west, east, rows)
+    count = values_ref.shape[0]
+    edges = [west, east]
+    position = count - 2
+    while len(edges) - 1 < count:
+        spans = len(edges) - 1
+        mids = [middle(kept_local_ref[position + i], edges[i], edges[i + 1], rows) for i in range(spans)]
+        edges = [e for pair in zip(edges, mids) for e in pair] + [edges[-1]]
+        position -= 2 * spans
+    for i in range(count):
+        values_ref[i] = edges[i]
+
+
+def power_of_two(n):
+    return n >= 2 and n & (n - 1) == 0
+
+
+def longitude_shards(h_cond, v_cond, confidence, teacher, grad_x, grad_y):
+    local_rows, slice_cols = h_cond.shape
+    maps = teacher.shape[0]
+    strips, panels = lax.axis_size("strip"), lax.axis_size("panel")
+    rows, lanes, width = local_rows * strips, 4 * local_rows * strips, slice_cols // strips
+    along = h_cond[None] * grad_x
+    flux = v_cond[None] * grad_y
+    load = confidence[None] * teacher - along - flux
+    small = jnp.stack([h_cond, v_cond, confidence], axis=0)
+
+    def padded(part):
+        return jnp.pad(part, ((0, rows - part.shape[0]), (0, 0), (0, 0)))
+
+    packed = jnp.concatenate([padded(small), padded(flux), padded(along), padded(load)], axis=0)
+    packed = jnp.transpose(packed, (2, 1, 0))
+    fields = lax.all_to_all(packed, "strip", 0, 1, tiled=True)
+    f32 = jnp.float32
+
+    def shape(*dims):
+        return jax.ShapeDtypeStruct(dims, f32)
+
+    segment, kept_local = pl.pallas_call(
+        functools.partial(local_kernel, rows=rows, maps=maps),
+        out_shape=(shape(2 * rows, lanes), shape(width - 1, rows, lanes)),
+    )(fields)
+    segments = lax.all_gather(segment, "strip")
+    segment, kept_strip = pl.pallas_call(
+        functools.partial(group_kernel, rows=rows),
+        out_shape=(shape(2 * rows, lanes), shape(strips - 1, rows, lanes)),
+    )(segments)
+    segments = lax.all_gather(segment, "panel")
+    position = jnp.stack([lax.axis_index("strip"), lax.axis_index("panel")]).astype(jnp.int32)
+    values = pl.pallas_call(
+        functools.partial(final_kernel, rows=rows, strips=strips, panels=panels),
+        out_shape=shape(width, rows, lanes),
+        in_specs=[pl.BlockSpec(memory_space=pltpu.SMEM)] + [pl.BlockSpec(memory_space=pltpu.VMEM)] * 3,
+        scratch_shapes=[pltpu.VMEM((panels - 1, rows, lanes), f32)],
+    )(position, segments, kept_local, kept_strip)
+    values = values[:, :, 3 * rows : 3 * rows + maps]
+    values = lax.all_to_all(values, "strip", 1, 0, tiled=True)
+    return jnp.transpose(values, (2, 1, 0))
+
+
+def shards(h_cond, v_cond, confidence, teacher, grad_x, grad_y):
+    strips, panels = lax.axis_size("strip"), lax.axis_size("panel")
+    rows, cols = h_cond.shape[0] * strips, h_cond.shape[1]
+    width = cols // strips
+    short = 4 * rows == 128 and 3 <= rows and teacher.shape[0] <= rows
+    even = cols % strips == 0 and all(power_of_two(n) for n in (strips, panels, width))
+    body = longitude_shards if short and even else latitude_shards
+    return body(h_cond, v_cond, confidence, teacher, grad_x, grad_y)
+
+
 def solution(mesh):
     in_specs = (
         P("strip", "panel"),

time: 1310 us -> 94 us (0.07)
  other arithmetic: 818 us -> 2.02 us
  local copies, waits for them, and re-layouts: 131 us -> 4.78 us
  matrix products: 97 us -> 0 us
  blocking collectives: 124 us -> 48.8 us
  waiting for transfers between devices: 77.8 us -> 6.77 us
  loops' own time: 32.6 us -> 0 us
  Pallas kernels: 0 us -> 23.7 us
  between operations: 15.2 us -> 0.11 us
    another operation x157 -> x2, other arithmetic: 809 us -> 1.27 us  [the longest x1 0.7 us: longitude_shards(): small = jnp.stack([h_cond, v_cond, confidence], axis=0)]
    all_gather x4 -> x0, waiting for transfers between devices: 76 us -> none  [carried_in(): pieces = jax.tree.map(lambda part: lax.all_gather(part, axis), value)]
    all_gather x4 -> x2, blocking collectives: 101 us -> 39.9 us  [the longest x1 33 us: longitude_shards(): segments = lax.all_gather(segment, 'strip')]
    another operation x140 -> x0, local copies, waits for them, and re-layouts: 60.9 us -> none  [the longest x70 39 us: merge_whole(): jax.scipy.linalg.cho_solve((factor, True), jnp.concatenate([upper[1].T, l...]
    another operation x180 -> x0, matrix products: 54.8 us -> none  [the longest x60 23.6 us: merge_whole(): jax.scipy.linalg.cho_solve((factor, True), jnp.concatenate([upper[1].T, l...]
    dot_general x63 -> x0, matrix products: 42.2 us -> none  [product(): jnp.dot(left, right, precision=HIGH, preferred_element_type=jnp.float32)]
    another operation x21 -> x0, loops' own time: 32.6 us -> none  [the longest x2 20.7 us: carried_in(): return lax.fori_loop(0, count - 1, turn, total)]
    dynamic_slice x44 -> x0, local copies, waits for them, and re-layouts: 24.2 us -> none  [the longest x21 11.8 us: turn(): longer = join(total, jax.tree.map(lambda part: part[position], pieces))]
  transfers between devices with their start and end apart: 5 -> 1, of which waited for: 4 -> 1; matrix products, arithmetic and copies ran while one was open for 0% -> 1% of each run, Pallas kernels for 0% -> 0%
where the time goes in v1:
time: 94 us; the launch traced here: 93.4 us
  blocking collectives  48.8 us (52%)
  Pallas kernels  23.7 us (25%)
  starting transfers between devices  7.31 us (8%)
  waiting for transfers between devices  6.77 us (7%)
  local copies, waits for them, and re-layouts  4.78 us (5%)
  other arithmetic  2.02 us (2%)
    all_gather x1, blocking collectives, longitude_shards(): segments = lax.all_gather(segment, 'strip')  33 us
    all_to_all x1, blocking collectives, longitude_shards(): values = lax.all_to_all(values, 'strip', 1, 0, tiled=True)  8.94 us
    pallas_call x1, Pallas kernels, longitude_shards(): pl.pallas_call(functools.partial(local_kernel, rows=rows, maps=maps), out...  8.07 us
    pallas_call x1, Pallas kernels, longitude_shards(): pl.pallas_call(functools.partial(group_kernel, rows=rows), out_shape=(sha...  7.92 us
    pallas_call x1, Pallas kernels, longitude_shards(): pl.pallas_call(functools.partial(final_kernel, rows=rows, strips=strips,...  7.67 us
    all_to_all x1, starting transfers between devices, longitude_shards(): fields = lax.all_to_all(packed, 'strip', 0, 1, tiled=True)  7.31 us
    all_gather x1, blocking collectives, longitude_shards(): segments = lax.all_gather(segment, 'panel')  6.89 us
    all_to_all x1, waiting for transfers between devices, longitude_shards(): fields = lax.all_to_all(packed, 'strip', 0, 1, tiled=True)  6.77 us
  transfers between devices with their start and end apart: 1, of which 1 were waited for; matrix products, arithmetic and copies ran while one was open for 1% of the time, Pallas kernels for 0%

profile of v1, /device:TPU:0, one launch (start us, length us, event | category | flops | bytes accessed | tf_op | source)
XLA Modules:
  0.0 93.4 jit_solution(6367736767747549249)
XLA Ops:
  0.0 0.0 copy-start.4
  0.0 0.0 copy-start.3
  0.0 0.0 copy-start.5
  0.0 0.7 copy-done.4
  0.7 0.0 copy-done.3
  0.7 0.0 copy-start
  0.7 0.0 copy-start.1
  0.7 0.0 copy-start.2
  0.7 0.7 select_maximum_fusion.3
  1.4 0.0 copy-done.5
  1.4 0.0 copy-done
  1.5 0.0 copy-done.1
  1.5 0.0 copy-done.2
  1.6 0.8 copy.19
  2.4 7.3 %all-to-all-start = ((f32[64,4,128]{2,1,0:T(4,128)}), f32[64,4,128]{2,1,0:T(4,128)S(1)}, u32[]{:S(2)}, u32[]{:S(2)}) async-start(f32[64,4,128]{2,1,0:T(4,128)} %copy.19), calls=%async_computation | async-start | bytes 262144 | tf_op jit(solution)/shard_map/all_to_all | solution.py:357
  9.7 0.6 pad_add_fusion.where_ref
  10.2 6.8 %all-to-all-done = f32[64,4,128]{2,1,0:T(4,128)S(1)} async-done(((f32[64,4,128]{2,1,0:T(4,128)}), f32[64,4,128]{2,1,0:T(4,128)S(1)}, u32[]{:S(2)}, u32[]{:S(2)}) %all-to-all-start) | async-done | bytes 131104 | tf_op jit(solution)/shard_map/all_to_all | solution.py:357
  17.0 0.7 copy.21
  17.8 8.1 %shard_map.64 = (f32[64,128]{1,0:T(8,128)}, f32[7,32,128]{2,1,0:T(8,128)}) custom-call(f32[8,32,128]{2,1,0:T(8,128)} %bitcast.39), custom_call_target="tpu_custom_call" | custom-call | tf_op jit(solution)/shard_map/pallas_call | solution.py:363
  25.8 33.0 %all-gather = f32[512,128]{1,0:T(8,128)} all-gather(f32[64,128]{1,0:T(8,128)} %get-tuple-element.9), channel_id=2, replica_groups=mesh['strip'=8,'panel'=4] {'strip'}, dimensions={0}, use_global_device_ids=true | all-gather | bytes 294912 | tf_op jit(solution)/shard_map/all_gather | solution.py:367
  58.8 7.9 %shard_map.65 = (f32[64,128]{1,0:T(8,128)}, f32[7,32,128]{2,1,0:T(8,128)}) custom-call(f32[8,64,128]{2,1,0:T(8,128)} %bitcast.36), custom_call_target="tpu_custom_call" | custom-call | tf_op jit(solution)/shard_map/pallas_call | solution.py:368
  66.7 6.9 %all-gather.1 = f32[256,128]{1,0:T(8,128)} all-gather(f32[64,128]{1,0:T(8,128)} %get-tuple-element.10), channel_id=3, replica_groups=mesh['strip'=8,'panel'=4] {'panel'}, dimensions={0}, use_global_device_ids=true | all-gather | bytes 163840 | tf_op jit(solution)/shard_map/all_gather | solution.py:372
  73.6 7.7 %shard_map.66 = f32[8,32,128]{2,1,0:T(8,128)} custom-call(s32[2]{0:T(128)} %pad_add_fusion.where_ref, f32[4,64,128]{2,1,0:T(8,128)} %bitcast.37, f32[7,32,128]{2,1,0:T(8,128)} %get-tuple-element.11.kept_local_ref, f32[7,32,128]{2,1,0:T(8,128)} %get-tuple-element.12.kept_strip_ref), custom_call_target="tpu_custom_call" | custom-call | tf_op jit(solution)/shard_map/pallas_call | solution.py:374
  81.3 1.0 %slice.4 = f32[8,32,16]{2,1,0:T(8,128)S(1)} slice(f32[8,32,128]{2,1,0:T(8,128)} %shard_map.66), slice={[0:8], [0:32], [96:112]} | slice | bytes 32768 | tf_op jit(solution)/shard_map/slice | solution.py:380
  82.3 0.1 copy.30
  82.4 0.1 reshape.5
  82.5 8.9 %all_to_all.36 = f32[8,1,512]{2,1,0:T(1,128)S(1)} all-to-all(f32[8,1,512]{2,1,0:T(1,128)S(1)} %reshape.5), channel_id=1, replica_groups=mesh['strip'=8,'panel'=4] {'strip'}, dimensions={0} | all-to-all | bytes 32768 | tf_op jit(solution)/shard_map/all_to_all | solution.py:381
  91.4 0.5 broadcast.34
  91.9 0.7 reduce
  92.6 0.1 reshape.6
  92.7 0.7 copy.24
  (7 shorter events, 0.1 us)
Async XLA Ops:
  0.0 0.7 copy-start.4
  0.0 0.7 copy-start.3
  0.0 1.4 %copy-start.5 = (f32[4,64]{1,0:T(4,128)S(1)}, f32[4,64]{1,0:T(4,128)}, u32[]{:S(2)}) copy-start(f32[4,64]{1,0:T(4,128)} %param.7) | copy-start | bytes 3076
  0.7 0.8 copy-start
  0.7 0.8 copy-start.1
  0.7 0.8 copy-start.2
  2.4 14.7 %all-to-all-start = ((f32[64,4,128]{2,1,0:T(4,128)}), f32[64,4,128]{2,1,0:T(4,128)S(1)}, u32[]{:S(2)}, u32[]{:S(2)}) async-start(f32[64,4,128]{2,1,0:T(4,128)} %copy.19), calls=%async_computation | async-start | bytes 262144 | tf_op jit(solution)/shard_map/all_to_all | solution.py:357

commit v2 on v1

--- a/solution.py
+++ b/solution.py
@@ -252,28 +252,15 @@
     return jnp.where(lane_block(x.shape, rows) == 3, x - product(x, right), 0.0)
 
 
-def descend(kept_ref, leaves, leaf, west, east, rows):
-    position, count = leaves - 2, 1
-    while count < leaves:
-        held = kept_ref[position + (leaf * count) // leaves]
-        mid = middle(held, west, east, rows)
-        go_east = ((leaf * 2 * count) // leaves) % 2 == 1
-        west, east = jnp.where(go_east, mid, west), jnp.where(go_east, east, mid)
-        count *= 2
-        position -= count
-    return west, east
-
-
-def local_kernel(fields_ref, segment_ref, kept_ref, *, rows, maps):
+def load_segments(fields_ref, rows, maps):
     count, _, lanes = fields_ref.shape
     shape = (rows, lanes)
     block = lane_block(shape, rows)
     lane = lax.broadcasted_iota(jnp.int32, shape, 1)
     row = lax.broadcasted_iota(jnp.int32, shape, 0)
     diag0, diag1, diag2 = lane == row, lane == row + rows, lane == row + 2 * rows
-    upper, lower = lane == row + rows + 1, lane == row + rows - 1
-    upper = jnp.logical_and(upper, block == 1)
-    lower = jnp.logical_and(lower, block == 1)
+    upper = jnp.logical_and(lane == row + rows + 1, block == 1)
+    lower = jnp.logical_and(lane == row + rows - 1, block == 1)
     load_lane = jnp.logical_and(lane >= 3 * rows, lane < 3 * rows + maps)
     tops, bottoms = [], []
     for j in range(count):
@@ -285,54 +272,112 @@
         va = jnp.broadcast_to(above[:, 1:2], shape)
         flux_above = pltpu.roll(above, 2 * rows, 1)
         along = pltpu.roll(f, rows, 1)
-        top = (
+        tops.append(
             jnp.where(diag1, h + va + v + w, 0.0)
             - jnp.where(upper, v, 0.0)
             - jnp.where(lower, va, 0.0)
             - jnp.where(diag2, h, 0.0)
             + jnp.where(load_lane, f + flux_above, 0.0)
         )
-        bottom = jnp.where(diag1, h, 0.0) - jnp.where(diag0, h, 0.0) + jnp.where(load_lane, along, 0.0)
-        tops.append(top)
-        bottoms.append(bottom)
-    top, bottom = merge_tree(tops, bottoms, rows, kept_ref)
-    segment_ref[0:rows] = top
-    segment_ref[rows : 2 * rows] = bottom
-
-
-def group_kernel(segments_ref, segment_ref, kept_ref, *, rows):
-    count = segments_ref.shape[0]
-    tops = [segments_ref[i, 0:rows] for i in range(count)]
-    bottoms = [segments_ref[i, rows : 2 * rows] for i in range(count)]
-    top, bottom = merge_tree(tops, bottoms, rows, kept_ref)
-    segment_ref[0:rows] = top
-    segment_ref[rows : 2 * rows] = bottom
-
-
-def final_kernel(
-    where_ref, segments_ref, kept_local_ref, kept_strip_ref, values_ref, kept_panel_ref, *, rows, strips, panels
+        bottoms.append(
+            jnp.where(diag1, h, 0.0) - jnp.where(diag0, h, 0.0) + jnp.where(load_lane, along, 0.0)
+        )
+    return tops, bottoms
+
+
+def partner_of(axis, step):
+    me = lax.axis_index(axis)
+    side = (me // (1 << step)) % 2
+    return me + (1 - 2 * side) * (1 << step), side
+
+
+def swap_blocks(axis, source_ref, target_ref, send, recv):
+    count, me = lax.axis_size(axis), lax.axis_index(axis)
+    copies = []
+    for step in range(1, count):
+        peer = (me + step) % count
+        copy = pltpu.make_async_remote_copy(
+            src_ref=source_ref.at[peer],
+            dst_ref=target_ref.at[me],
+            send_sem=send.at[step - 1],
+            recv_sem=recv.at[step - 1],
+            device_id={axis: peer},
+            device_id_type=pl.DeviceIdType.MESH,
+        )
+        copy.start()
+        copies.append(copy)
+    target_ref[me] = source_ref[me]
+    for copy in copies:
+        copy.wait()
+
+
+def solve_kernel(
+    parts_ref, out_ref, got_ref, fields_ref, local_ref, path_ref, mine_ref, theirs_ref, done_ref,
+    send_in, recv_in, send_merge, recv_merge, send_out, recv_out, *, rows, maps, strip_steps, panel_steps,
 ):
-    lanes = segments_ref.shape[2]
+    strips, me = lax.axis_size("strip"), lax.axis_index("strip")
+    width, _, lanes = fields_ref.shape
+    local_rows = rows // strips
+    hops = [("strip", s) for s in range(strip_steps)] + [("panel", s) for s in range(panel_steps)]
+    barrier = pltpu.get_barrier_semaphore()
+    greeted = [("strip", (me + s) % strips) for s in range(1, strips)]
+    greeted += [("panel", partner_of("panel", s)[0]) for s in range(panel_steps)]
+    for axis, peer in greeted:
+        pl.semaphore_signal(barrier, inc=1, device_id={axis: peer}, device_id_type=pl.DeviceIdType.MESH)
+    pl.semaphore_wait(barrier, len(greeted))
+
+    swap_blocks("strip", parts_ref, got_ref, send_in, recv_in)
+    for s in range(strips):
+        for j in range(width):
+            fields_ref[j, s * local_rows : (s + 1) * local_rows] = got_ref[
+                s, j * local_rows : (j + 1) * local_rows
+            ]
+    tops, bottoms = load_segments(fields_ref, rows, maps)
+    top, bottom = merge_tree(tops, bottoms, rows, local_ref)
+    for level, (axis, step) in enumerate(hops):
+        partner, side = partner_of(axis, step)
+        mine_ref[level, 0:rows] = top
+        mine_ref[level, rows : 2 * rows] = bottom
+        copy = pltpu.make_async_remote_copy(
+            src_ref=mine_ref.at[level],
+            dst_ref=theirs_ref.at[level],
+            send_sem=send_merge.at[level],
+            recv_sem=recv_merge.at[level],
+            device_id={axis: partner},
+            device_id_type=pl.DeviceIdType.MESH,
+        )
+        copy.start()
+        copy.wait()
+        other_top, other_bottom = theirs_ref[level, 0:rows], theirs_ref[level, rows : 2 * rows]
+        east = side == 1
+        pair_tops = [jnp.where(east, other_top, top), jnp.where(east, top, other_top)]
+        pair_bottoms = [jnp.where(east, other_bottom, bottom), jnp.where(east, bottom, other_bottom)]
+        solved, new_tops, new_bottoms = merge_segments(pair_tops, pair_bottoms, rows)
+        path_ref[level] = solved[0]
+        top, bottom = new_tops[0], new_bottoms[0]
+
     block = lane_block((rows, lanes), rows)
-    tops = [segments_ref[i, 0:rows] for i in range(panels)]
-    bottoms = [segments_ref[i, rows : 2 * rows] for i in range(panels)]
-    top, bottom = merge_tree(tops, bottoms, rows, kept_panel_ref)
     wrap = pltpu.roll(top, lanes - rows, 1) + pltpu.roll(bottom, rows, 1)
     closing = top + bottom + jnp.where(block == 1, wrap, 0.0)
     first = eliminate_column([closing], rows, 4)[0]
-    first = jnp.where(block == 3, first, 0.0)
-    west, east = descend(kept_panel_ref, panels, where_ref[1], first, first, rows)
-    west, east = descend(kept_strip_ref, strips, where_ref[0], west, east, rows)
-    count = values_ref.shape[0]
+    west = east = jnp.where(block == 3, first, 0.0)
+    for level in reversed(range(len(hops))):
+        _, side = partner_of(*hops[level])
+        mid = middle(path_ref[level], west, east, rows)
+        west, east = jnp.where(side == 1, mid, west), jnp.where(side == 1, east, mid)
     edges = [west, east]
-    position = count - 2
-    while len(edges) - 1 < count:
+    position = width - 2
+    while len(edges) - 1 < width:
         spans = len(edges) - 1
-        mids = [middle(kept_local_ref[position + i], edges[i], edges[i + 1], rows) for i in range(spans)]
+        mids = [middle(local_ref[position + i], edges[i], edges[i + 1], rows) for i in range(spans)]
         edges = [e for pair in zip(edges, mids) for e in pair] + [edges[-1]]
         position -= 2 * spans
-    for i in range(count):
-        values_ref[i] = edges[i]
+    for s in range(strips):
+        for j in range(width):
+            done_ref[s, j * local_rows : (j + 1) * local_rows] = edges[j][
+                s * local_rows : (s + 1) * local_rows
+            ]
+    swap_blocks("strip", done_ref, out_ref, send_out, recv_out)
 
 
 def power_of_two(n):
@@ -344,6 +389,8 @@
     maps = teacher.shape[0]
     strips, panels = lax.axis_size("strip"), lax.axis_size("panel")
     rows, lanes, width = local_rows * strips, 4 * local_rows * strips, slice_cols // strips
+    strip_steps, panel_steps = strips.bit_length() - 1, panels.bit_length() - 1
+    levels = strip_steps + panel_steps
     along = h_cond[None] * grad_x
     flux = v_cond[None] * grad_y
     load = confidence[None] * teacher - along - flux
@@ -353,32 +400,34 @@
         return jnp.pad(part, ((0, rows - part.shape[0]), (0, 0), (0, 0)))
 
     packed = jnp.concatenate([padded(small), padded(flux), padded(along), padded(load)], axis=0)
-    packed = jnp.transpose(packed, (2, 1, 0))
-    fields = lax.all_to_all(packed, "strip", 0, 1, tiled=True)
+    packed = jnp.transpose(packed, (2, 1, 0)).reshape(strips, width * local_rows, lanes)
     f32 = jnp.float32
-
-    def shape(*dims):
-        return jax.ShapeDtypeStruct(dims, f32)
-
-    segment, kept_local = pl.pallas_call(
-        functools.partial(local_kernel, rows=rows, maps=maps),
-        out_shape=(shape(2 * rows, lanes), shape(width - 1, rows, lanes)),
-    )(fields)
-    segments = lax.all_gather(segment, "strip")
-    segment, kept_strip = pl.pallas_call(
-        functools.partial(group_kernel, rows=rows),
-        out_shape=(shape(2 * rows, lanes), shape(strips - 1, rows, lanes)),
-    )(segments)
-    segments = lax.all_gather(segment, "panel")
-    position = jnp.stack([lax.axis_index("strip"), lax.axis_index("panel")]).astype(jnp.int32)
+    dma = pltpu.SemaphoreType.DMA
     values = pl.pallas_call(
-        functools.partial(final_kernel, rows=rows, strips=strips, panels=panels),
-        out_shape=shape(width, rows, lanes),
-        in_specs=[pl.BlockSpec(memory_space=pltpu.SMEM)] + [pl.BlockSpec(memory_space=pltpu.VMEM)] * 3,
-        scratch_shapes=[pltpu.VMEM((panels - 1, rows, lanes), f32)],
-    )(position, segments, kept_local, kept_strip)
-    values = values[:, :, 3 * rows : 3 * rows + maps]
-    values = lax.all_to_all(values, "strip", 1, 0, tiled=True)
+        functools.partial(
+            solve_kernel, rows=rows, maps=maps, strip_steps=strip_steps, panel_steps=panel_steps
+        ),
+        out_shape=jax.ShapeDtypeStruct((strips, width * local_rows, lanes), f32),
+        in_specs=[pl.BlockSpec(memory_space=pltpu.VMEM)],
+        out_specs=pl.BlockSpec(memory_space=pltpu.VMEM),
+        scratch_shapes=[
+            pltpu.VMEM((strips, width * local_rows, lanes), f32),
+            pltpu.VMEM((width, rows, lanes), f32),
+            pltpu.VMEM((width - 1, rows, lanes), f32),
+            pltpu.VMEM((levels, rows, lanes), f32),
+            pltpu.VMEM((levels, 2 * rows, lanes), f32),
+            pltpu.VMEM((levels, 2 * rows, lanes), f32),
+            pltpu.VMEM((strips, width * local_rows, lanes), f32),
+            dma((strips - 1,)),
+            dma((strips - 1,)),
+            dma((levels,)),
+            dma((levels,)),
+            dma((strips - 1,)),
+            dma((strips - 1,)),
+        ],
+        compiler_params=pltpu.CompilerParams(collective_id=0, has_side_effects=True),
+    )(packed)
+    values = values.reshape(slice_cols, local_rows, lanes)[:, :, 3 * rows : 3 * rows + maps]
     return jnp.transpose(values, (2, 1, 0))
 
 

time: 94 us -> 49.3 us (0.52)
  blocking collectives: 48.8 us -> 0 us
  Pallas kernels: 23.7 us -> 44.9 us
  starting transfers between devices: 7.31 us -> 0 us
  waiting for transfers between devices: 6.77 us -> 0 us
  other arithmetic: 2.02 us -> 0.07 us
    all_gather x2 -> x0, blocking collectives: 39.9 us -> none  [the longest x1 33 us: longitude_shards(): segments = lax.all_gather(segment, 'strip')]
    pallas_call x3 -> x1, Pallas kernels: 23.7 us -> 44.9 us  [longitude_shards(): pl.pallas_call(functools.partial(solve_kernel, rows=rows, maps=maps, stri...]
    all_to_all x1 -> x0, blocking collectives: 8.94 us -> none  [longitude_shards(): values = lax.all_to_all(values, 'strip', 1, 0, tiled=True)]
    all_to_all x1 -> x0, starting transfers between devices: 7.31 us -> none  [longitude_shards(): fields = lax.all_to_all(packed, 'strip', 0, 1, tiled=True)]
    all_to_all x1 -> x0, waiting for transfers between devices: 6.77 us -> none  [longitude_shards(): fields = lax.all_to_all(packed, 'strip', 0, 1, tiled=True)]
    all_to_all x4 -> x0, local copies, waits for them, and re-layouts: 1.27 us -> none  [the longest x2 0.75 us: longitude_shards(): fields = lax.all_to_all(packed, 'strip', 0, 1, tiled=True)]
    unnamed x17 -> x16, local copies, waits for them, and re-layouts: 0.96 us -> 2.17 us
  transfers between devices with their start and end apart: 1 -> 0, of which waited for: 1 -> 0; matrix products, arithmetic and copies ran while one was open for 1% -> 0% of each run, Pallas kernels for 0% -> 0%
where the time goes in v2:
time: 49.3 us; the launch traced here: 49 us
  Pallas kernels  44.9 us (91%)
  local copies, waits for them, and re-layouts  3.97 us (8%)
    pallas_call x1, Pallas kernels, longitude_shards(): pl.pallas_call(functools.partial(solve_kernel, rows=rows, maps=maps, stri...  44.9 us
    unnamed x16, local copies, waits for them, and re-layouts  2.17 us
    slice x1, local copies, waits for them, and re-layouts, longitude_shards(): values.reshape(slice_cols, local_rows, lanes)  1.03 us

profile of v2, /device:TPU:0, one launch (start us, length us, event | category | flops | bytes accessed | tf_op | source)
XLA Modules:
  0.0 49.0 jit_solution(18180155162574583357)
XLA Ops:
  0.0 0.0 copy-start.5
  0.0 0.0 copy-start.4
  0.0 0.0 copy-start.3
  0.0 0.0 copy-start.2
  0.0 0.7 %copy-done.4 = f32[4,64]{1,0:T(4,128)S(1)} copy-done((f32[4,64]{1,0:T(4,128)S(1)}, f32[4,64]{1,0:T(4,128)}, u32[]{:S(2)}) %copy-start.4) | copy-done | bytes 1048
  0.7 0.0 copy-done.5
  0.7 0.0 copy-done.3
  0.7 0.0 copy-start
  0.7 0.0 copy-start.1
  0.8 0.0 copy-done.2
  0.8 0.7 %copy-done = f32[16,4,64]{2,1,0:T(4,128)S(1)} copy-done((f32[16,4,64]{2,1,0:T(4,128)S(1)}, f32[16,4,64]{2,1,0:T(4,128)}, u32[]{:S(2)}) %copy-start) | copy-done | bytes 16408
  1.5 0.0 copy-done.1
  1.6 0.8 %copy.7 = f32[64,4,128]{2,1,0:T(4,128)} copy(f32[64,4,128]{0,1,2:T(4,128)S(1)} %fusion) | data formatting | bytes 262144 | tf_op jit(solution)/shard_map/transpose | solution.py:403
  2.3 44.9 %shard_map.64 = f32[8,32,128]{2,1,0:T(8,128)} custom-call(f32[8,32,128]{2,1,0:T(8,128)} %bitcast.17), custom_call_target="tpu_custom_call" | custom-call | tf_op jit(solution)/shard_map/pallas_call | solution.py:406
  47.2 1.0 %slice.4 = f32[64,4,16]{2,1,0:T(4,128)S(1)} slice(f32[64,4,128]{2,1,0:T(4,128)} %bitcast.18), slice={[0:64], [0:4], [96:112]} | slice | bytes 32768 | tf_op jit(solution)/shard_map/slice | solution.py:430
  48.3 0.7 %copy.9 = f32[64,4,16]{0,1,2:T(4,128)} copy(f32[64,4,16]{2,1,0:T(4,128)S(1)} %slice.4) | data formatting | bytes 32768
  (6 shorter events, 0.1 us)
Async XLA Ops:
  0.0 0.7 %copy-start.5 = (f32[4,64]{1,0:T(4,128)S(1)}, f32[4,64]{1,0:T(4,128)}, u32[]{:S(2)}) copy-start(f32[4,64]{1,0:T(4,128)} %param.7) | copy-start | bytes 3076
  0.0 0.7 %copy-start.4 = (f32[4,64]{1,0:T(4,128)S(1)}, f32[4,64]{1,0:T(4,128)}, u32[]{:S(2)}) copy-start(f32[4,64]{1,0:T(4,128)} %param.6) | copy-start | bytes 3076
  0.0 0.7 %copy-start.3 = (f32[4,64]{1,0:T(4,128)S(1)}, f32[4,64]{1,0:T(4,128)}, u32[]{:S(2)}) copy-start(f32[4,64]{1,0:T(4,128)} %param.8) | copy-start | bytes 3076
  0.0 0.8 %copy-start.2 = (f32[16,4,64]{2,1,0:T(4,128)S(1)}, f32[16,4,64]{2,1,0:T(4,128)}, u32[]{:S(2)}) copy-start(f32[16,4,64]{2,1,0:T(4,128)} %param.11) | copy-start | bytes 49156
  0.7 0.8 %copy-start = (f32[16,4,64]{2,1,0:T(4,128)S(1)}, f32[16,4,64]{2,1,0:T(4,128)}, u32[]{:S(2)}) copy-start(f32[16,4,64]{2,1,0:T(4,128)} %param.9) | copy-start | bytes 49156
  0.7 0.8 %copy-start.1 = (f32[16,4,64]{2,1,0:T(4,128)S(1)}, f32[16,4,64]{2,1,0:T(4,128)}, u32[]{:S(2)}) copy-start(f32[16,4,64]{2,1,0:T(4,128)} %param.10) | copy-start | bytes 49156

commit v3 on v2

--- a/solution.py
+++ b/solution.py
@@ -217,23 +217,27 @@
 
 def merge_segments(tops, bottoms, rows):
     pairs = len(tops) // 2
-    group = max(1, 4 // pairs)
-    lanes = tops[0].shape[1]
-    block = lane_block(tops[0].shape, rows)
-    zero = jnp.zeros((rows, lanes), jnp.float32)
+    group = rows // 2 if pairs == 1 else rows // 4
     solved = eliminate_column(
         [bottoms[2 * i] + tops[2 * i + 1] for i in range(pairs)], rows, group
     )
+    new_tops, new_bottoms = reduce_segments(solved, tops[::2], bottoms[1::2], rows)
+    return solved, new_tops, new_bottoms
+
+
+def reduce_segments(solved, wests, easts, rows):
+    lanes = solved[0].shape[1]
+    block = lane_block(solved[0].shape, rows)
+    zero = jnp.zeros((rows, lanes), jnp.float32)
     new_tops, new_bottoms = [], []
-    for i, x in enumerate(solved):
+    for x, west, east in zip(solved, wests, easts):
         x_top = jnp.where(block == 0, 0.0, jnp.where(block == 1, pltpu.roll(x, rows, 1), x))
         x_bottom = jnp.where(block == 2, 0.0, jnp.where(block == 1, pltpu.roll(x, lanes - rows, 1), x))
         right = jnp.concatenate([x_bottom, zero, x_top, zero], axis=0)
-        west, east = tops[2 * i], bottoms[2 * i + 1]
         change = product(jnp.concatenate([west, east], axis=0), right)
         new_tops.append(jnp.where(block == 2, 0.0, west) - change[:rows])
         new_bottoms.append(jnp.where(block == 0, 0.0, east) - change[rows:])
-    return solved, new_tops, new_bottoms
+    return new_tops, new_bottoms
 
 
 def merge_tree(tops, bottoms, rows, kept_ref):
@@ -336,30 +340,36 @@
     top, bottom = merge_tree(tops, bottoms, rows, local_ref)
     for level, (axis, step) in enumerate(hops):
         partner, side = partner_of(axis, step)
-        mine_ref[level, 0:rows] = top
-        mine_ref[level, rows : 2 * rows] = bottom
-        copy = pltpu.make_async_remote_copy(
-            src_ref=mine_ref.at[level],
-            dst_ref=theirs_ref.at[level],
-            send_sem=send_merge.at[level],
-            recv_sem=recv_merge.at[level],
-            device_id={axis: partner},
-            device_id_type=pl.DeviceIdType.MESH,
-        )
-        copy.start()
-        copy.wait()
-        other_top, other_bottom = theirs_ref[level, 0:rows], theirs_ref[level, rows : 2 * rows]
+        mine_ref[level, 0] = top
+        mine_ref[level, 1] = bottom
+        copies = []
+        for order, half in enumerate((1 - side, side)):
+            copy = pltpu.make_async_remote_copy(
+                src_ref=mine_ref.at[level, half],
+                dst_ref=theirs_ref.at[level, half],
+                send_sem=send_merge.at[level, order],
+                recv_sem=recv_merge.at[level, order],
+                device_id={axis: partner},
+                device_id_type=pl.DeviceIdType.MESH,
+            )
+            copy.start()
+            copies.append(copy)
         east = side == 1
-        pair_tops = [jnp.where(east, other_top, top), jnp.where(east, top, other_top)]
-        pair_bottoms = [jnp.where(east, other_bottom, bottom), jnp.where(east, bottom, other_bottom)]
-        solved, new_tops, new_bottoms = merge_segments(pair_tops, pair_bottoms, rows)
+        copies[0].wait()
+        facing = jnp.where(east, top, bottom) + theirs_ref[level, side]
+        solved = eliminate_column([facing], rows, rows // 2)
         path_ref[level] = solved[0]
+        copies[1].wait()
+        far = theirs_ref[level, 1 - side]
+        new_tops, new_bottoms = reduce_segments(
+            solved, [jnp.where(east, far, top)], [jnp.where(east, bottom, far)], rows
+        )
         top, bottom = new_tops[0], new_bottoms[0]
 
     block = lane_block((rows, lanes), rows)
     wrap = pltpu.roll(top, lanes - rows, 1) + pltpu.roll(bottom, rows, 1)
     closing = top + bottom + jnp.where(block == 1, wrap, 0.0)
-    first = eliminate_column([closing], rows, 4)[0]
+    first = eliminate_column([closing], rows, rows // 2)[0]
     west = east = jnp.where(block == 3, first, 0.0)
     for level in reversed(range(len(hops))):
         _, side = partner_of(*hops[level])
@@ -372,11 +382,13 @@
         mids = [middle(local_ref[position + i], edges[i], edges[i + 1], rows) for i in range(spans)]
         edges = [e for pair in zip(edges, mids) for e in pair] + [edges[-1]]
         position -= 2 * spans
+    slot = lax.broadcasted_iota(jnp.int32, (rows, lanes), 1) // maps
+    packed = jnp.zeros((rows, lanes), jnp.float32)
+    for j in range(width):
+        moved = pltpu.roll(edges[j], (j * maps + rows) % lanes, 1)
+        packed = jnp.where(slot == j, moved, packed)
     for s in range(strips):
-        for j in range(width):
-            done_ref[s, j * local_rows : (j + 1) * local_rows] = edges[j][
-                s * local_rows : (s + 1) * local_rows
-            ]
+        done_ref[s] = packed[s * local_rows : (s + 1) * local_rows]
     swap_blocks("strip", done_ref, out_ref, send_out, recv_out)
 
 
@@ -407,7 +419,7 @@
         functools.partial(
             solve_kernel, rows=rows, maps=maps, strip_steps=strip_steps, panel_steps=panel_steps
         ),
-        out_shape=jax.ShapeDtypeStruct((strips, width * local_rows, lanes), f32),
+        out_shape=jax.ShapeDtypeStruct((strips, local_rows, lanes), f32),
         in_specs=[pl.BlockSpec(memory_space=pltpu.VMEM)],
         out_specs=pl.BlockSpec(memory_space=pltpu.VMEM),
         scratch_shapes=[
@@ -415,27 +427,27 @@
             pltpu.VMEM((width, rows, lanes), f32),
             pltpu.VMEM((width - 1, rows, lanes), f32),
             pltpu.VMEM((levels, rows, lanes), f32),
-            pltpu.VMEM((levels, 2 * rows, lanes), f32),
-            pltpu.VMEM((levels, 2 * rows, lanes), f32),
-            pltpu.VMEM((strips, width * local_rows, lanes), f32),
+            pltpu.VMEM((levels, 2, rows, lanes), f32),
+            pltpu.VMEM((levels, 2, rows, lanes), f32),
+            pltpu.VMEM((strips, local_rows, lanes), f32),
             dma((strips - 1,)),
             dma((strips - 1,)),
-            dma((levels,)),
-            dma((levels,)),
+            dma((levels, 2)),
+            dma((levels, 2)),
             dma((strips - 1,)),
             dma((strips - 1,)),
         ],
         compiler_params=pltpu.CompilerParams(collective_id=0, has_side_effects=True),
     )(packed)
-    values = values.reshape(slice_cols, local_rows, lanes)[:, :, 3 * rows : 3 * rows + maps]
-    return jnp.transpose(values, (2, 1, 0))
+    values = values[:, :, : width * maps].reshape(strips, local_rows, width, maps)
+    return jnp.transpose(values, (3, 1, 0, 2)).reshape(maps, local_rows, slice_cols)
 
 
 def shards(h_cond, v_cond, confidence, teacher, grad_x, grad_y):
     strips, panels = lax.axis_size("strip"), lax.axis_size("panel")
     rows, cols = h_cond.shape[0] * strips, h_cond.shape[1]
     width = cols // strips
-    short = 4 * rows == 128 and 3 <= rows and teacher.shape[0] <= rows
+    short = 4 * rows == 128 and 3 <= rows and teacher.shape[0] <= rows and width * teacher.shape[0] <= 4 * rows
     even = cols % strips == 0 and all(power_of_two(n) for n in (strips, panels, width))
     body = longitude_shards if short and even else latitude_shards
     return body(h_cond, v_cond, confidence, teacher, grad_x, grad_y)

time: 49.3 us -> 43 us (0.87)
  Pallas kernels: 44.9 us -> 38.7 us
    pallas_call x1, Pallas kernels: 44.9 us -> 38.7 us  [longitude_shards(): pl.pallas_call(functools.partial(solve_kernel, rows=rows, maps=maps, stri...]
    reshape x0 -> x3, local copies, waits for them, and re-layouts: none -> 1.53 us  [the longest x2 0.83 us: longitude_shards(): values[:, :, :width * maps].reshape(strips, local_rows, width, maps)]
    slice x1 -> x0, local copies, waits for them, and re-layouts: 1.03 us -> none  [longitude_shards(): values.reshape(slice_cols, local_rows, lanes)]
    unnamed x16 -> x15, local copies, waits for them, and re-layouts: 2.17 us -> 1.46 us
where the time goes in v3:
time: 43 us; the launch traced here: 42.6 us
  Pallas kernels  38.7 us (90%)
  local copies, waits for them, and re-layouts  3.76 us (9%)
    pallas_call x1, Pallas kernels, longitude_shards(): pl.pallas_call(functools.partial(solve_kernel, rows=rows, maps=maps, stri...  38.7 us
    unnamed x15, local copies, waits for them, and re-layouts  1.46 us

profile of v3, /device:TPU:0, one launch (start us, length us, event | category | flops | bytes accessed | tf_op | source)
XLA Modules:
  0.0 42.6 jit_solution(4792102043440251056)
XLA Ops:
  0.0 0.0 copy-start.5
  0.0 0.0 copy-start.4
  0.0 0.0 copy-start.3
  0.0 0.0 copy-start.2
  0.0 0.7 %copy-done.4 = f32[4,64]{1,0:T(4,128)S(1)} copy-done((f32[4,64]{1,0:T(4,128)S(1)}, f32[4,64]{1,0:T(4,128)}, u32[]{:S(2)}) %copy-start.4) | copy-done | bytes 1048
  0.7 0.0 copy-done.5
  0.7 0.0 copy-done.3
  0.7 0.0 copy-start
  0.7 0.0 copy-start.1
  0.8 0.0 copy-done.2
  0.8 0.7 %copy-done = f32[16,4,64]{2,1,0:T(4,128)S(1)} copy-done((f32[16,4,64]{2,1,0:T(4,128)S(1)}, f32[16,4,64]{2,1,0:T(4,128)}, u32[]{:S(2)}) %copy-start) | copy-done | bytes 16408
  1.5 0.0 copy-done.1
  1.6 0.8 %copy.9 = f32[64,4,128]{2,1,0:T(4,128)} copy(f32[64,4,128]{0,1,2:T(4,128)S(1)} %fusion) | data formatting | bytes 262144 | tf_op jit(solution)/shard_map/transpose | solution.py:415
  2.3 38.7 %shard_map.64 = f32[8,4,128]{2,1,0:T(4,128)} custom-call(f32[8,32,128]{2,1,0:T(8,128)} %bitcast.20), custom_call_target="tpu_custom_call" | custom-call | tf_op jit(solution)/shard_map/pallas_call | solution.py:418
  41.1 0.8 %reshape.13 = f32[8,4,8,16]{3,2,1,0:T(8,128)S(1)} reshape(f32[8,4,128]{2,1,0:T(4,128)} %shard_map.64) | data formatting | bytes 32768 | tf_op jit(solution)/shard_map/reshape | solution.py:442
  41.9 0.7 %copy.11 = f32[16,4,64]{2,1,0:T(4,128)} copy(f32[16,4,64]{0,2,1:T(8,128)S(1)} %bitcast.21) | data formatting | bytes 32768 | tf_op jit(solution)/shard_map/reshape | solution.py:443
  (7 shorter events, 0.1 us)
Async XLA Ops:
  0.0 0.7 %copy-start.5 = (f32[4,64]{1,0:T(4,128)S(1)}, f32[4,64]{1,0:T(4,128)}, u32[]{:S(2)}) copy-start(f32[4,64]{1,0:T(4,128)} %param.7) | copy-start | bytes 3076
  0.0 0.7 %copy-start.4 = (f32[4,64]{1,0:T(4,128)S(1)}, f32[4,64]{1,0:T(4,128)}, u32[]{:S(2)}) copy-start(f32[4,64]{1,0:T(4,128)} %param.6) | copy-start | bytes 3076
  0.0 0.7 %copy-start.3 = (f32[4,64]{1,0:T(4,128)S(1)}, f32[4,64]{1,0:T(4,128)}, u32[]{:S(2)}) copy-start(f32[4,64]{1,0:T(4,128)} %param.8) | copy-start | bytes 3076
  0.0 0.8 %copy-start.2 = (f32[16,4,64]{2,1,0:T(4,128)S(1)}, f32[16,4,64]{2,1,0:T(4,128)}, u32[]{:S(2)}) copy-start(f32[16,4,64]{2,1,0:T(4,128)} %param.11) | copy-start | bytes 49156
  0.7 0.8 %copy-start = (f32[16,4,64]{2,1,0:T(4,128)S(1)}, f32[16,4,64]{2,1,0:T(4,128)}, u32[]{:S(2)}) copy-start(f32[16,4,64]{2,1,0:T(4,128)} %param.9) | copy-start | bytes 49156
  0.7 0.8 %copy-start.1 = (f32[16,4,64]{2,1,0:T(4,128)S(1)}, f32[16,4,64]{2,1,0:T(4,128)}, u32[]{:S(2)}) copy-start(f32[16,4,64]{2,1,0:T(4,128)} %param.10) | copy-start | bytes 49156

commit v4 on v3

--- a/solution.py
+++ b/solution.py
@@ -248,12 +248,6 @@
             kept_ref[position] = x
             position += 1
     return tops[0], bottoms[0]
-
-
-def middle(x, west, east, rows):
-    zero = jnp.zeros_like(x)
-    right = jnp.concatenate([west, zero, east, zero], axis=0)
-    return jnp.where(lane_block(x.shape, rows) == 3, x - product(x, right), 0.0)
 
 
 def load_segments(fields_ref, rows, maps):
@@ -289,6 +283,31 @@
     return tops, bottoms
 
 
+def compose(maps_in, x, east, rows):
+    block = lane_block(maps_in.shape, rows)
+    x = jnp.where(lane_block(x.shape, rows) == 1, 0.0, x)
+    zero = jnp.zeros_like(x)
+    right = jnp.concatenate([jnp.where(east, x, 0.0), zero, jnp.where(east, 0.0, x), zero], axis=0)
+    return jnp.where(block == jnp.where(east, 0, 2), 0.0, maps_in) - product(maps_in, right)
+
+
+def local_maps(local_ref, width, rows, lanes):
+    row = lax.broadcasted_iota(jnp.int32, (rows, lanes), 0)
+    lane = lax.broadcasted_iota(jnp.int32, (rows, lanes), 1)
+    stacks = [jnp.where(lane == row, -1.0, 0.0)] * width
+    position = 0
+    while len(stacks) > 1:
+        merged = []
+        for i in range(len(stacks) // 2):
+            x = local_ref[position]
+            position += 1
+            west = compose(stacks[2 * i], x, False, rows)
+            east = compose(stacks[2 * i + 1], x, True, rows)
+            merged.append(jnp.concatenate([west, east], axis=0))
+        stacks = merged
+    return stacks[0]
+
+
 def partner_of(axis, step):
     me = lax.axis_index(axis)
     side = (me // (1 << step)) % 2
@@ -355,10 +374,14 @@
             copy.start()
             copies.append(copy)
         east = side == 1
+        if level == 0:
+            path_ref[...] = local_maps(local_ref, width, rows, lanes)
+        else:
+            path_ref[...] = compose(path_ref[...], *last, rows)
         copies[0].wait()
         facing = jnp.where(east, top, bottom) + theirs_ref[level, side]
         solved = eliminate_column([facing], rows, rows // 2)
-        path_ref[level] = solved[0]
+        last = (solved[0], east)
         copies[1].wait()
         far = theirs_ref[level, 1 - side]
         new_tops, new_bottoms = reduce_segments(
@@ -370,22 +393,14 @@
     wrap = pltpu.roll(top, lanes - rows, 1) + pltpu.roll(bottom, rows, 1)
     closing = top + bottom + jnp.where(block == 1, wrap, 0.0)
     first = eliminate_column([closing], rows, rows // 2)[0]
-    west = east = jnp.where(block == 3, first, 0.0)
-    for level in reversed(range(len(hops))):
-        _, side = partner_of(*hops[level])
-        mid = middle(path_ref[level], west, east, rows)
-        west, east = jnp.where(side == 1, mid, west), jnp.where(side == 1, east, mid)
-    edges = [west, east]
-    position = width - 2
-    while len(edges) - 1 < width:
-        spans = len(edges) - 1
-        mids = [middle(local_ref[position + i], edges[i], edges[i + 1], rows) for i in range(spans)]
-        edges = [e for pair in zip(edges, mids) for e in pair] + [edges[-1]]
-        position -= 2 * spans
+    first = jnp.where(block == 3, first, 0.0)
+    zero = jnp.zeros_like(first)
+    maps_all = compose(path_ref[...], *last, rows)
+    values = maps_all - product(maps_all, jnp.concatenate([first, zero, first, zero], axis=0))
     slot = lax.broadcasted_iota(jnp.int32, (rows, lanes), 1) // maps
     packed = jnp.zeros((rows, lanes), jnp.float32)
     for j in range(width):
-        moved = pltpu.roll(edges[j], (j * maps + rows) % lanes, 1)
+        moved = pltpu.roll(values[j * rows : (j + 1) * rows], (j * maps + rows) % lanes, 1)
         packed = jnp.where(slot == j, moved, packed)
     for s in range(strips):
         done_ref[s] = packed[s * local_rows : (s + 1) * local_rows]
@@ -426,7 +441,7 @@
             pltpu.VMEM((strips, width * local_rows, lanes), f32),
             pltpu.VMEM((width, rows, lanes), f32),
             pltpu.VMEM((width - 1, rows, lanes), f32),
-            pltpu.VMEM((levels, rows, lanes), f32),
+            pltpu.VMEM((width * rows, lanes), f32),
             pltpu.VMEM((levels, 2, rows, lanes), f32),
             pltpu.VMEM((levels, 2, rows, lanes), f32),
             pltpu.VMEM((strips, local_rows, lanes), f32),

time: 43 us -> 42.3 us (0.984)
  Pallas kernels: 38.7 us -> 38.1 us
    pallas_call x1, Pallas kernels: 38.7 us -> 38.1 us  [longitude_shards(): pl.pallas_call(functools.partial(solve_kernel, rows=rows, maps=maps, stri...]
where the time goes in v4:
time: 42.3 us; the launch traced here: 42 us
  Pallas kernels  38.1 us (90%)
  local copies, waits for them, and re-layouts  3.76 us (9%)
    pallas_call x1, Pallas kernels, longitude_shards(): pl.pallas_call(functools.partial(solve_kernel, rows=rows, maps=maps, stri...  38.1 us
    unnamed x15, local copies, waits for them, and re-layouts  1.46 us

profile of v4, /device:TPU:0, one launch (start us, length us, event | category | flops | bytes accessed | tf_op | source)
XLA Modules:
  0.0 42.0 jit_solution(3017377732978953463)
XLA Ops:
  0.0 0.0 copy-start.5
  0.0 0.0 copy-start.4
  0.0 0.0 copy-start.3
  0.0 0.0 copy-start.2
  0.0 0.7 %copy-done.4 = f32[4,64]{1,0:T(4,128)S(1)} copy-done((f32[4,64]{1,0:T(4,128)S(1)}, f32[4,64]{1,0:T(4,128)}, u32[]{:S(2)}) %copy-start.4) | copy-done | bytes 1048
  0.7 0.0 copy-done.5
  0.7 0.0 copy-done.3
  0.7 0.0 copy-start
  0.7 0.0 copy-start.1
  0.8 0.0 copy-done.2
  0.8 0.7 %copy-done = f32[16,4,64]{2,1,0:T(4,128)S(1)} copy-done((f32[16,4,64]{2,1,0:T(4,128)S(1)}, f32[16,4,64]{2,1,0:T(4,128)}, u32[]{:S(2)}) %copy-start) | copy-done | bytes 16408
  1.5 0.0 copy-done.1
  1.6 0.8 %copy.9 = f32[64,4,128]{2,1,0:T(4,128)} copy(f32[64,4,128]{0,1,2:T(4,128)S(1)} %fusion) | data formatting | bytes 262144 | tf_op jit(solution)/shard_map/transpose | solution.py:430
  2.3 38.1 %shard_map.64 = f32[8,4,128]{2,1,0:T(4,128)} custom-call(f32[8,32,128]{2,1,0:T(8,128)} %bitcast.20), custom_call_target="tpu_custom_call" | custom-call | tf_op jit(solution)/shard_map/pallas_call | solution.py:433
  40.5 0.8 %reshape.13 = f32[8,4,8,16]{3,2,1,0:T(8,128)S(1)} reshape(f32[8,4,128]{2,1,0:T(4,128)} %shard_map.64) | data formatting | bytes 32768 | tf_op jit(solution)/shard_map/reshape | solution.py:457
  41.3 0.7 %copy.11 = f32[16,4,64]{2,1,0:T(4,128)} copy(f32[16,4,64]{0,2,1:T(8,128)S(1)} %bitcast.21) | data formatting | bytes 32768 | tf_op jit(solution)/shard_map/reshape | solution.py:458
  (7 shorter events, 0.1 us)
Async XLA Ops:
  0.0 0.7 %copy-start.5 = (f32[4,64]{1,0:T(4,128)S(1)}, f32[4,64]{1,0:T(4,128)}, u32[]{:S(2)}) copy-start(f32[4,64]{1,0:T(4,128)} %param.7) | copy-start | bytes 3076
  0.0 0.7 %copy-start.4 = (f32[4,64]{1,0:T(4,128)S(1)}, f32[4,64]{1,0:T(4,128)}, u32[]{:S(2)}) copy-start(f32[4,64]{1,0:T(4,128)} %param.6) | copy-start | bytes 3076
  0.0 0.7 %copy-start.3 = (f32[4,64]{1,0:T(4,128)S(1)}, f32[4,64]{1,0:T(4,128)}, u32[]{:S(2)}) copy-start(f32[4,64]{1,0:T(4,128)} %param.8) | copy-start | bytes 3076
  0.0 0.8 %copy-start.2 = (f32[16,4,64]{2,1,0:T(4,128)S(1)}, f32[16,4,64]{2,1,0:T(4,128)}, u32[]{:S(2)}) copy-start(f32[16,4,64]{2,1,0:T(4,128)} %param.11) | copy-start | bytes 49156
  0.7 0.8 %copy-start = (f32[16,4,64]{2,1,0:T(4,128)S(1)}, f32[16,4,64]{2,1,0:T(4,128)}, u32[]{:S(2)}) copy-start(f32[16,4,64]{2,1,0:T(4,128)} %param.9) | copy-start | bytes 49156
  0.7 0.8 %copy-start.1 = (f32[16,4,64]{2,1,0:T(4,128)S(1)}, f32[16,4,64]{2,1,0:T(4,128)}, u32[]{:S(2)}) copy-start(f32[16,4,64]{2,1,0:T(4,128)} %param.10) | copy-start | bytes 49156
